TPU v7x, 32 devices: a whole 2x2x4 slice. The times are simulated.
32 devices in a mesh: grp: 2 (over x), had: 16 (over z, y, core).
Axes of the slice: x: 2, y: 2, z: 4, core: 2. Of those that a mesh axis runs over, the one named last changes fastest.
Arguments:
- source_slabs: bfloat16 [512, 128, 128], P(('grp', 'had')), parts along dimension 0, may hold values from -6 to 6
- sink_slabs: bfloat16 [512, 128, 128], P(('grp', 'had')), parts along dimension 0, may hold values from -6 to 6
- perambulators: bfloat16 [4, 2, 128, 128], P('grp'), parts along dimension 0, may hold values from -0.5 to 0.5
- send_pick: int32 [32, 16], P(('grp', 'had')), parts along dimension 0, may hold values from 0 to 15
- graph_slot: int32 [32, 512, 2], P(('grp', 'had')), parts along dimension 0, may hold values from 0 to 15
- graph_sink: int32 [32, 512, 2], P(('grp', 'had')), parts along dimension 0, may hold values from 0 to 15
- graph_count: int32 [32], P(('grp', 'had')), parts along dimension 0, may hold values from 64 to 512, as said below
- pair_list: int32 [256, 2], P(('grp', 'had')), parts along dimension 0, may hold values from 0 to 15
Outputs:
- edge_matrices: bfloat16 [32, 128, 128], P(('grp', 'had')), parts along dimension 0
- pair_products: bfloat16 [256, 128, 128], P(('grp', 'had')), parts along dimension 0
There are 2 independent parts, one for each index of `grp`. A program takes and returns all parts, laid end to end along the dimension named above; each array names one. Nothing has to cross between parts.
Inputs may be any that keep to these rules, and one draw needn't show every extreme that they name: Some reader uses all 512 graph slots; slots from graph_count on are unused.
All inputs are finite; a program needn't handle non-finite values.
Results may differ from a plain program's by a relative error of at most 0.012.
Values may be sent and summed in bfloat16 or wider, within the bound.
A program may use at most 64 MiB of HBM per device.

v0:
```python
import math
import jax
import jax.numpy as jnp
from jax import lax
from jax.sharding import PartitionSpec as P


def shards(
    source_slabs,
    sink_slabs,
    perambulators,
    send_pick,
    graph_slot,
    graph_sink,
    graph_count,
    pair_list,
):
    my_index = lax.axis_index("had")
    evecs = source_slabs.shape[1]
    per_device = source_slabs.shape[0]
    root_scale = 1.0 / math.sqrt(evecs)
    edge_scale = 1.0 / math.sqrt(evecs * graph_slot.shape[1])
    timeslice = my_index * per_device // evecs
    local_peram = lax.dynamic_index_in_dim(perambulators, timeslice, 0, keepdims=False)
    first_turn = jnp.einsum(
        "xa,jab->xjb", local_peram[0], source_slabs, preferred_element_type=jnp.float32
    ).astype(jnp.bfloat16)
    pick_row = send_pick[0]
    second_turn = jnp.einsum(
        "xjb,yb->xjy", first_turn, local_peram[1], preferred_element_type=jnp.float32
    ).astype(jnp.bfloat16)
    outgoing = jnp.take(second_turn, pick_row, axis=1)
    received = lax.all_to_all(outgoing, "had", split_axis=1, concat_axis=1, tiled=True)
    graph_rows = graph_slot.shape[1]
    block_width = min(64, graph_rows)
    slot_table = graph_slot[0]
    sink_table = graph_sink[0]
    graph_total = graph_count[0]

    def factor(slots, sinks):
        gathered = jnp.take(received, slots, axis=1)
        resident = jnp.take(sink_slabs, sinks, axis=0)
        product = jnp.einsum("gxb,agb->gxa", resident, gathered, preferred_element_type=jnp.float32)
        return (product * root_scale).astype(jnp.bfloat16)

    def accumulate(block_index, running_sum):
        offset = block_index * block_width
        slots = lax.dynamic_slice_in_dim(slot_table, offset, block_width, 0)
        sinks = lax.dynamic_slice_in_dim(sink_table, offset, block_width, 0)
        is_valid = (offset + jnp.arange(block_width, dtype=jnp.int32) < graph_total).astype(
            jnp.bfloat16
        )
        left_side = factor(slots[:, 0], sinks[:, 0]) * is_valid[:, None, None]
        right_side = factor(slots[:, 1], sinks[:, 1])
        return running_sum + jnp.einsum(
            "gxa,gay->xy", left_side, right_side, preferred_element_type=jnp.float32
        )

    block_count = (graph_total + block_width - 1) // block_width
    summed = lax.fori_loop(0, block_count, accumulate, jnp.zeros((evecs, evecs), jnp.float32))
    edge_local = (summed * edge_scale).astype(jnp.bfloat16)[None]
    left_ids = pair_list[:, 0]
    right_ids = pair_list[:, 1]
    shard_rows = lax.all_gather(edge_local, "had", axis=0, tiled=True)
    row_ids = jnp.arange(shard_rows.shape[0], dtype=jnp.int32)
    left_select = (left_ids[:, None] == row_ids[None, :]).astype(jnp.bfloat16)
    right_select = (right_ids[:, None] == row_ids[None, :]).astype(jnp.bfloat16)
    left_part = jnp.einsum(
        "pn,nxy->pxy", left_select, shard_rows, preferred_element_type=jnp.float32
    )
    right_part = jnp.einsum(
        "pn,nxy->pxy", right_select, shard_rows, preferred_element_type=jnp.float32
    )
    left_edges = left_part.astype(jnp.bfloat16)
    right_edges = right_part.astype(jnp.bfloat16)
    product = jnp.einsum(
        "pxa,pay->pxy", left_edges, right_edges, preferred_element_type=jnp.float32
    )
    pair_products = (product * root_scale).astype(jnp.bfloat16)
    return (edge_local, pair_products)


def solution(mesh):
    return jax.shard_map(
        shards,
        mesh=mesh,
        in_specs=(
            P(("grp", "had"), None, None),
            P(("grp", "had"), None, None),
            P("grp", None, None, None),
            P(("grp", "had"), None),
            P(("grp", "had"), None, None),
            P(("grp", "had"), None, None),
            P(("grp", "had")),
            P(("grp", "had"), None),
        ),
        out_specs=(P(("grp", "had"), None, None), P(("grp", "had"), None, None)),
        check_vma=False,
    )
```

profile of v0, /device:TPU:0, one launch (start us, length us, event | category | flops | bytes accessed | tf_op | source)
XLA Modules:
  0.0 210.6 jit_solution(10187311681063074676)
XLA Ops:
  0.6 0.0 copy-start
  0.7 0.7 fusion.45
  1.4 0.7 compare_and_fusion.4
  2.0 0.0 copy-done
  2.1 0.0 copy-start.2
  2.1 0.0 copy-start.1
  2.1 1.3 convolution_convert_fusion
  3.4 0.6 gather_fusion.4
  4.1 0.9 select_bitcast_fusion
  5.0 7.4 %all-to-all-start = ((bf16[128,16,128]{2,0,1:T(8,128)(2,1)}), bf16[128,16,128]{2,0,1:T(8,128)(2,1)S(1)}, u32[]{:S(2)}, u32[]{:S(2)}) async-start(bf16[128,16,128]{2,0,1:T(8,128)(2,1)} %select_bitcast_fusion), calls=%async_computation | async-start | bytes 1048576 | tf_op jit(solution)/shard_map/all_to_all | solution.py:33
  13.1 0.0 copy-done.2
  13.1 13.6 %all-to-all-done = bf16[128,16,128]{2,0,1:T(8,128)(2,1)S(1)} async-done(((bf16[128,16,128]{2,0,1:T(8,128)(2,1)}), bf16[128,16,128]{2,0,1:T(8,128)(2,1)S(1)}, u32[]{:S(2)}, u32[]{:S(2)}) %all-to-all-start) | async-done | bytes 524320 | tf_op jit(solution)/shard_map/all_to_all | solution.py:33
  26.7 0.0 copy-done.1
  26.7 81.4 %while.10 = (s32[]{:T(128)}, f32[128,128]{1,0:T(8,128)S(1)}, s32[]{:T(128)}, s32[512,2]{0,1:T(2,128)}, bf16[16,128,128]{2,1,0:T(8,128)(2,1)S(1)}, /*index=5*/s32...) while((s32[]{:T(128)}, f32[128,128]{1,0:T(8,128)S(1)}, ...), condition=%wide.region_1.4_spmd, body=%wide.region_0.3_spmd.sunk | while | flops 814765760 | bytes 29514672 | solution.py:60
  26.7 0.8 constant_dynamic-slice_fusion.3
  27.5 2.1 %gather_fusion = bf16[64,128,128]{2,1,0:T(8,128)(2,1)} fusion(bf16[128,16,128]{2,0,1:T(8,128)(2,1)S(1)} %get-tuple-element.188, s32[1024]{0:T(1024)S(1)} %pad_clamp_fusion.9), kind=kCustom, calls=%fused_computation.3.clone.clone.1 | custom fusion | bytes 4194560 | tf_op jit(solution)/shard_map/while/body/jit(_take)/gather | solution.py:41
  29.7 2.1 %gather_fusion.1 = bf16[64,128,128]{2,1,0:T(8,128)(2,1)} fusion(bf16[16,128,128]{2,1,0:T(8,128)(2,1)S(1)} %get-tuple-element.186, s32[1024]{0:T(1024)S(1)} %pad_clamp_fusion.10), kind=kCustom, calls=%fused_computation.2.clone.clone.1 | custom fusion | bytes 4194560 | tf_op jit(solution)/shard_map/while/body/jit(_take)/gather | solution.py:42
  31.8 5.2 %multiply_convert_fusion.4 = bf16[64,128,128]{2,1,0:T(8,128)(2,1)} fusion(bf16[64,128,128]{2,1,0:T(8,128)(2,1)} %gather_fusion, bf16[64,128,128]{2,1,0:T(8,128)(2,1)} %gather_fusion.1, pred[64]{0:T(512)(128)(4,1)S(1)} %get-tuple-element.152, pred[64]{0:T(512)(128)(4,1)S(1)} %get-tuple-element.153), kind=kOutput, calls=%fused_computation.5.clone.1 | convolution fusion | flops 272629760 | bytes 6291584 | tf_op jit(solution)/shard_map/while/body/gxb,agb->gxa/dot_general | solution.py:43
  37.0 2.1 %gather_fusion.2 = bf16[64,128,128]{2,1,0:T(8,128)(2,1)} fusion(bf16[128,16,128]{2,0,1:T(8,128)(2,1)S(1)} %get-tuple-element.188, s32[1024]{0:T(1024)S(1)} %pad_clamp_fusion.11), kind=kCustom, calls=%fused_computation.1.clone.clone.1 | custom fusion | bytes 4194560 | tf_op jit(solution)/shard_map/while/body/jit(_take)/gather | solution.py:41
  39.1 2.1 %gather_fusion.3 = bf16[64,128,128]{2,1,0:T(8,128)(2,1)} fusion(bf16[16,128,128]{2,1,0:T(8,128)(2,1)S(1)} %get-tuple-element.186, s32[1024]{0:T(1024)S(1)} %pad_clamp_fusion.12), kind=kCustom, calls=%fused_computation.clone.clone.1 | custom fusion | bytes 4194560 | tf_op jit(solution)/shard_map/while/body/jit(_take)/gather | solution.py:42
  41.3 0.6 compare_convert_fusion.2
  41.9 5.1 %fusion.64 = f32[128,128]{1,0:T(8,128)S(1)} fusion(f32[128,128]{1,0:T(8,128)S(1)} %get-tuple-element.171, bf16[64,128,128]{2,1,0:T(8,128)(2,1)} %multiply_convert_fusion.4, bf16[64,128,128]{2,1,0:T(8,128)(2,1)} %gather_fusion.2, bf16[64,128,128]{2,1,0:T(8,128)(2,1)} %gather_fusion.3, pred[64]{0:T(512)(128)(4,1)S(1)} %get-tuple-element.156, ...), kind=kOutput, calls=%fused_computation.20.clone.1 | convolution fusion | flops 542130176 | bytes 6422784 | tf_op jit(solution)/shard_map/while/body/gxa,gay->xy/dot_general | solution.py:55
  47.1 0.8 constant_dynamic-slice_fusion.3
  47.9 2.1 %gather_fusion = bf16[64,128,128]{2,1,0:T(8,128)(2,1)} fusion(bf16[128,16,128]{2,0,1:T(8,128)(2,1)S(1)} %get-tuple-element.188, s32[1024]{0:T(1024)S(1)} %pad_clamp_fusion.9), kind=kCustom, calls=%fused_computation.3.clone.clone.1 | custom fusion | bytes 4194560 | tf_op jit(solution)/shard_map/while/body/jit(_take)/gather | solution.py:41
  50.0 2.1 %gather_fusion.1 = bf16[64,128,128]{2,1,0:T(8,128)(2,1)} fusion(bf16[16,128,128]{2,1,0:T(8,128)(2,1)S(1)} %get-tuple-element.186, s32[1024]{0:T(1024)S(1)} %pad_clamp_fusion.10), kind=kCustom, calls=%fused_computation.2.clone.clone.1 | custom fusion | bytes 4194560 | tf_op jit(solution)/shard_map/while/body/jit(_take)/gather | solution.py:42
  52.1 5.2 %multiply_convert_fusion.4 = bf16[64,128,128]{2,1,0:T(8,128)(2,1)} fusion(bf16[64,128,128]{2,1,0:T(8,128)(2,1)} %gather_fusion, bf16[64,128,128]{2,1,0:T(8,128)(2,1)} %gather_fusion.1, pred[64]{0:T(512)(128)(4,1)S(1)} %get-tuple-element.152, pred[64]{0:T(512)(128)(4,1)S(1)} %get-tuple-element.153), kind=kOutput, calls=%fused_computation.5.clone.1 | convolution fusion | flops 272629760 | bytes 6291584 | tf_op jit(solution)/shard_map/while/body/gxb,agb->gxa/dot_general | solution.py:43
  57.4 2.1 %gather_fusion.2 = bf16[64,128,128]{2,1,0:T(8,128)(2,1)} fusion(bf16[128,16,128]{2,0,1:T(8,128)(2,1)S(1)} %get-tuple-element.188, s32[1024]{0:T(1024)S(1)} %pad_clamp_fusion.11), kind=kCustom, calls=%fused_computation.1.clone.clone.1 | custom fusion | bytes 4194560 | tf_op jit(solution)/shard_map/while/body/jit(_take)/gather | solution.py:41
  59.5 2.1 %gather_fusion.3 = bf16[64,128,128]{2,1,0:T(8,128)(2,1)} fusion(bf16[16,128,128]{2,1,0:T(8,128)(2,1)S(1)} %get-tuple-element.186, s32[1024]{0:T(1024)S(1)} %pad_clamp_fusion.12), kind=kCustom, calls=%fused_computation.clone.clone.1 | custom fusion | bytes 4194560 | tf_op jit(solution)/shard_map/while/body/jit(_take)/gather | solution.py:42
  61.6 0.6 compare_convert_fusion.2
  62.3 5.1 %fusion.64 = f32[128,128]{1,0:T(8,128)S(1)} fusion(f32[128,128]{1,0:T(8,128)S(1)} %get-tuple-element.171, bf16[64,128,128]{2,1,0:T(8,128)(2,1)} %multiply_convert_fusion.4, bf16[64,128,128]{2,1,0:T(8,128)(2,1)} %gather_fusion.2, bf16[64,128,128]{2,1,0:T(8,128)(2,1)} %gather_fusion.3, pred[64]{0:T(512)(128)(4,1)S(1)} %get-tuple-element.156, ...), kind=kOutput, calls=%fused_computation.20.clone.1 | convolution fusion | flops 542130176 | bytes 6422784 | tf_op jit(solution)/shard_map/while/body/gxa,gay->xy/dot_general | solution.py:55
  67.4 0.8 constant_dynamic-slice_fusion.3
  68.2 2.1 %gather_fusion = bf16[64,128,128]{2,1,0:T(8,128)(2,1)} fusion(bf16[128,16,128]{2,0,1:T(8,128)(2,1)S(1)} %get-tuple-element.188, s32[1024]{0:T(1024)S(1)} %pad_clamp_fusion.9), kind=kCustom, calls=%fused_computation.3.clone.clone.1 | custom fusion | bytes 4194560 | tf_op jit(solution)/shard_map/while/body/jit(_take)/gather | solution.py:41
  70.4 2.1 %gather_fusion.1 = bf16[64,128,128]{2,1,0:T(8,128)(2,1)} fusion(bf16[16,128,128]{2,1,0:T(8,128)(2,1)S(1)} %get-tuple-element.186, s32[1024]{0:T(1024)S(1)} %pad_clamp_fusion.10), kind=kCustom, calls=%fused_computation.2.clone.clone.1 | custom fusion | bytes 4194560 | tf_op jit(solution)/shard_map/while/body/jit(_take)/gather | solution.py:42
  72.5 5.2 %multiply_convert_fusion.4 = bf16[64,128,128]{2,1,0:T(8,128)(2,1)} fusion(bf16[64,128,128]{2,1,0:T(8,128)(2,1)} %gather_fusion, bf16[64,128,128]{2,1,0:T(8,128)(2,1)} %gather_fusion.1, pred[64]{0:T(512)(128)(4,1)S(1)} %get-tuple-element.152, pred[64]{0:T(512)(128)(4,1)S(1)} %get-tuple-element.153), kind=kOutput, calls=%fused_computation.5.clone.1 | convolution fusion | flops 272629760 | bytes 6291584 | tf_op jit(solution)/shard_map/while/body/gxb,agb->gxa/dot_general | solution.py:43
  77.7 2.1 %gather_fusion.2 = bf16[64,128,128]{2,1,0:T(8,128)(2,1)} fusion(bf16[128,16,128]{2,0,1:T(8,128)(2,1)S(1)} %get-tuple-element.188, s32[1024]{0:T(1024)S(1)} %pad_clamp_fusion.11), kind=kCustom, calls=%fused_computation.1.clone.clone.1 | custom fusion | bytes 4194560 | tf_op jit(solution)/shard_map/while/body/jit(_take)/gather | solution.py:41
  79.8 2.1 %gather_fusion.3 = bf16[64,128,128]{2,1,0:T(8,128)(2,1)} fusion(bf16[16,128,128]{2,1,0:T(8,128)(2,1)S(1)} %get-tuple-element.186, s32[1024]{0:T(1024)S(1)} %pad_clamp_fusion.12), kind=kCustom, calls=%fused_computation.clone.clone.1 | custom fusion | bytes 4194560 | tf_op jit(solution)/shard_map/while/body/jit(_take)/gather | solution.py:42
  82.0 0.6 compare_convert_fusion.2
  82.6 5.1 %fusion.64 = f32[128,128]{1,0:T(8,128)S(1)} fusion(f32[128,128]{1,0:T(8,128)S(1)} %get-tuple-element.171, bf16[64,128,128]{2,1,0:T(8,128)(2,1)} %multiply_convert_fusion.4, bf16[64,128,128]{2,1,0:T(8,128)(2,1)} %gather_fusion.2, bf16[64,128,128]{2,1,0:T(8,128)(2,1)} %gather_fusion.3, pred[64]{0:T(512)(128)(4,1)S(1)} %get-tuple-element.156, ...), kind=kOutput, calls=%fused_computation.20.clone.1 | convolution fusion | flops 542130176 | bytes 6422784 | tf_op jit(solution)/shard_map/while/body/gxa,gay->xy/dot_general | solution.py:55
  87.8 0.8 constant_dynamic-slice_fusion.3
  88.6 2.1 %gather_fusion = bf16[64,128,128]{2,1,0:T(8,128)(2,1)} fusion(bf16[128,16,128]{2,0,1:T(8,128)(2,1)S(1)} %get-tuple-element.188, s32[1024]{0:T(1024)S(1)} %pad_clamp_fusion.9), kind=kCustom, calls=%fused_computation.3.clone.clone.1 | custom fusion | bytes 4194560 | tf_op jit(solution)/shard_map/while/body/jit(_take)/gather | solution.py:41
  90.7 2.1 %gather_fusion.1 = bf16[64,128,128]{2,1,0:T(8,128)(2,1)} fusion(bf16[16,128,128]{2,1,0:T(8,128)(2,1)S(1)} %get-tuple-element.186, s32[1024]{0:T(1024)S(1)} %pad_clamp_fusion.10), kind=kCustom, calls=%fused_computation.2.clone.clone.1 | custom fusion | bytes 4194560 | tf_op jit(solution)/shard_map/while/body/jit(_take)/gather | solution.py:42
  92.8 5.2 %multiply_convert_fusion.4 = bf16[64,128,128]{2,1,0:T(8,128)(2,1)} fusion(bf16[64,128,128]{2,1,0:T(8,128)(2,1)} %gather_fusion, bf16[64,128,128]{2,1,0:T(8,128)(2,1)} %gather_fusion.1, pred[64]{0:T(512)(128)(4,1)S(1)} %get-tuple-element.152, pred[64]{0:T(512)(128)(4,1)S(1)} %get-tuple-element.153), kind=kOutput, calls=%fused_computation.5.clone.1 | convolution fusion | flops 272629760 | bytes 6291584 | tf_op jit(solution)/shard_map/while/body/gxb,agb->gxa/dot_general | solution.py:43
  98.1 2.1 %gather_fusion.2 = bf16[64,128,128]{2,1,0:T(8,128)(2,1)} fusion(bf16[128,16,128]{2,0,1:T(8,128)(2,1)S(1)} %get-tuple-element.188, s32[1024]{0:T(1024)S(1)} %pad_clamp_fusion.11), kind=kCustom, calls=%fused_computation.1.clone.clone.1 | custom fusion | bytes 4194560 | tf_op jit(solution)/shard_map/while/body/jit(_take)/gather | solution.py:41
  100.2 2.1 %gather_fusion.3 = bf16[64,128,128]{2,1,0:T(8,128)(2,1)} fusion(bf16[16,128,128]{2,1,0:T(8,128)(2,1)S(1)} %get-tuple-element.186, s32[1024]{0:T(1024)S(1)} %pad_clamp_fusion.12), kind=kCustom, calls=%fused_computation.clone.clone.1 | custom fusion | bytes 4194560 | tf_op jit(solution)/shard_map/while/body/jit(_take)/gather | solution.py:42
  102.3 0.6 compare_convert_fusion.2
  103.0 5.1 %fusion.64 = f32[128,128]{1,0:T(8,128)S(1)} fusion(f32[128,128]{1,0:T(8,128)S(1)} %get-tuple-element.171, bf16[64,128,128]{2,1,0:T(8,128)(2,1)} %multiply_convert_fusion.4, bf16[64,128,128]{2,1,0:T(8,128)(2,1)} %gather_fusion.2, bf16[64,128,128]{2,1,0:T(8,128)(2,1)} %gather_fusion.3, pred[64]{0:T(512)(128)(4,1)S(1)} %get-tuple-element.156, ...), kind=kOutput, calls=%fused_computation.20.clone.1 | convolution fusion | flops 542130176 | bytes 6422784 | tf_op jit(solution)/shard_map/while/body/gxa,gay->xy/dot_general | solution.py:55
  108.1 0.6 fusion.50
  108.7 100.1 %all-gather = bf16[2048,128]{1,0:T(8,128)(2,1)S(1)} all-gather(bf16[128,128]{1,0:T(8,128)(2,1)S(1)} %multiply_convert_fusion.2), channel_id=2, replica_groups=mesh['grp'=2,'had'=16] {'had'}, dimensions={0}, use_global_device_ids=true | all-gather | bytes 557056 | tf_op jit(solution)/shard_map/all_gather | solution.py:64
  208.8 0.4 fusion.35
  209.2 0.4 fusion.37
  209.6 0.9 fusion.34
  (28 shorter events, 0.2 us)
Async XLA Ops:
  0.6 1.4 copy-start
  2.1 11.0 %copy-start.2 = (s32[8,2]{0,1:T(2,128)S(1)}, s32[8,2]{0,1:T(2,128)}, u32[]{:S(2)}) copy-start(s32[8,2]{0,1:T(2,128)} %param.21) | copy-start | bytes 196
  2.1 24.6 %copy-start.1 = (bf16[16,128,128]{2,1,0:T(8,128)(2,1)S(1)}, bf16[16,128,128]{2,1,0:T(8,128)(2,1)}, u32[]{:S(2)}) copy-start(bf16[16,128,128]{2,1,0:T(8,128)(2,1)} %param.15) | copy-start | bytes 1572868
  5.0 21.7 %all-to-all-start = ((bf16[128,16,128]{2,0,1:T(8,128)(2,1)}), bf16[128,16,128]{2,0,1:T(8,128)(2,1)S(1)}, u32[]{:S(2)}, u32[]{:S(2)}) async-start(bf16[128,16,128]{2,0,1:T(8,128)(2,1)} %select_bitcast_fusion), calls=%async_computation | async-start | bytes 1048576 | tf_op jit(solution)/shard_map/all_to_all | solution.py:33
where the time goes:
time: 211 us
  blocking collectives  100 us (47%)
  matrix products  44.2 us (21%)
  local copies, waits for them, and re-layouts  37.9 us (18%)
  waiting for transfers between devices  13.6 us (6%)
  starting transfers between devices  7.41 us (4%)
  other arithmetic  5.68 us (3%)
    all_gather x1, blocking collectives, shards(): shard_rows = lax.all_gather(edge_local, 'had', axis=0, tiled=True)  100 us
    dot_general x4, matrix products, factor(): jnp.einsum('gxb,agb->gxa', resident, gathered, preferred_element_type=jnp...  20.8 us
    dot_general x4, matrix products, accumulate(): jnp.einsum('gxa,gay->xy', left_side, right_side, preferred_element_type=j...  20.3 us
    gather x8, local copies, waits for them, and re-layouts, factor(): resident = jnp.take(sink_slabs, sinks, axis=0)  17.1 us
    gather x8, local copies, waits for them, and re-layouts, factor(): gathered = jnp.take(received, slots, axis=1)  17.1 us
    all_to_all x1, waiting for transfers between devices, shards(): lax.all_to_all(outgoing, 'had', split_axis=1, concat_axis=1, tiled=True)  13.6 us
    all_to_all x1, starting transfers between devices, shards(): lax.all_to_all(outgoing, 'had', split_axis=1, concat_axis=1, tiled=True)  7.41 us
  transfers between devices with their start and end apart: 1, of which 1 were waited for; matrix products, arithmetic and copies ran while one was open for 0% of the time, Pallas kernels for 0%

commit v1 on v0

--- a/solution.py
+++ b/solution.py
@@ -30,7 +30,10 @@
         "xjb,yb->xjy", first_turn, local_peram[1], preferred_element_type=jnp.float32
     ).astype(jnp.bfloat16)
     outgoing = jnp.take(second_turn, pick_row, axis=1)
-    received = lax.all_to_all(outgoing, "had", split_axis=1, concat_axis=1, tiled=True)
+    received = jnp.concatenate(
+        lax.all_to_all(jnp.stack(jnp.split(outgoing, lax.axis_size("had"), axis=1)), "had", 0, 0),
+        axis=1,
+    )
     graph_rows = graph_slot.shape[1]
     block_width = min(64, graph_rows)
     slot_table = graph_slot[0]

time: 211 us -> 220 us (1.043)
  local copies, waits for them, and re-layouts: 37.9 us -> 47.6 us
    unnamed x6 -> x21, local copies, waits for them, and re-layouts: 0.02 us -> 9.1 us
where the time goes in v1:
time: 220 us; the launch traced here: 219 us
  blocking collectives  100 us (45%)
  local copies, waits for them, and re-layouts  47.6 us (22%)
  matrix products  44.2 us (20%)
  waiting for transfers between devices  13.6 us (6%)
  starting transfers between devices  7.41 us (3%)
  other arithmetic  4.88 us (2%)
    all_gather x1, blocking collectives, shards(): shard_rows = lax.all_gather(edge_local, 'had', axis=0, tiled=True)  100 us
    dot_general x4, matrix products, factor(): jnp.einsum('gxb,agb->gxa', resident, gathered, preferred_element_type=jnp...  20.8 us
    dot_general x4, matrix products, accumulate(): jnp.einsum('gxa,gay->xy', left_side, right_side, preferred_element_type=j...  20.3 us
    gather x8, local copies, waits for them, and re-layouts, factor(): resident = jnp.take(sink_slabs, sinks, axis=0)  17.1 us
    gather x8, local copies, waits for them, and re-layouts, factor(): gathered = jnp.take(received, slots, axis=1)  17.1 us
    all_to_all x1, waiting for transfers between devices, shards(): lax.all_to_all(jnp.stack(jnp.split(outgoing, lax.axis_size('had'), axis=1...  13.6 us
    unnamed x21, local copies, waits for them, and re-layouts  9.1 us
    all_to_all x1, starting transfers between devices, shards(): lax.all_to_all(jnp.stack(jnp.split(outgoing, lax.axis_size('had'), axis=1...  7.41 us
  transfers between devices with their start and end apart: 1, of which 1 were waited for; matrix products, arithmetic and copies ran while one was open for 0% of the time, Pallas kernels for 0%

profile of v1, /device:TPU:0, one launch (start us, length us, event | category | flops | bytes accessed | tf_op | source)
XLA Modules:
  0.0 219.4 jit_solution(14772571454816507399)
XLA Ops:
  0.6 0.0 copy-start
  0.7 0.7 fusion.61
  1.4 0.7 compare_and_fusion.4
  2.1 1.3 convolution_convert_fusion
  3.3 0.0 copy-start.2
  3.3 0.0 copy-start.1
  3.3 0.6 gather_fusion.4
  4.0 0.1 select_bitcast_fusion
  4.1 0.6 fusion.54
  4.7 0.6 fusion.53
  5.3 0.6 fusion.52
  5.9 0.6 fusion.51
  6.5 0.6 fusion.50
  7.2 0.6 fusion.49
  7.8 0.6 fusion.48
  8.4 0.6 fusion.47
  9.0 0.6 fusion.46
  9.6 0.6 fusion.45
  10.2 0.6 fusion.44
  10.8 0.6 fusion.43
  11.4 0.6 fusion.42
  12.0 0.6 fusion.41
  12.6 0.6 fusion.40
  13.2 0.6 fusion.39
  13.8 7.4 %all-to-all-start = ((bf16[16,128,1,128]{3,1,2,0:T(8,128)(2,1)}), bf16[16,128,1,128]{3,1,2,0:T(8,128)(2,1)S(1)}, u32[]{:S(2)}, u32[]{:S(2)}) async-start(bf16[16,128,1,128]{3,1,2,0:T(8,128)(2,1)} %fusion.39), calls=%async_computation | async-start | bytes 1048576 | tf_op jit(solution)/shard_map/all_to_all | solution.py:34
  21.9 13.6 %all-to-all-done = bf16[16,128,1,128]{3,1,2,0:T(8,128)(2,1)S(1)} async-done(((bf16[16,128,1,128]{3,1,2,0:T(8,128)(2,1)}), bf16[16,128,1,128]{3,1,2,0:T(8,128)(2,1)S(1)}, u32[]{:S(2)}, u32[]{:S(2)}) %all-to-all-start) | async-done | bytes 524320 | tf_op jit(solution)/shard_map/all_to_all | solution.py:34
  35.5 81.4 %while.10 = (s32[]{:T(128)}, f32[128,128]{1,0:T(8,128)S(1)}, s32[]{:T(128)}, s32[512,2]{0,1:T(2,128)}, bf16[16,128,128]{2,1,0:T(8,128)(2,1)S(1)}, /*index=5*/s32...) while((s32[]{:T(128)}, f32[128,128]{1,0:T(8,128)S(1)}, ...), condition=%wide.region_1.4_spmd, body=%wide.region_0.3_spmd.sunk | while | flops 814765760 | bytes 29514672 | solution.py:63
  35.5 0.8 constant_dynamic-slice_fusion.3
  36.3 2.1 gather_fusion
  38.5 2.1 gather_fusion.1
  40.6 5.2 %multiply_convert_fusion.4 = bf16[64,128,128]{2,1,0:T(8,128)(2,1)} fusion(bf16[64,128,128]{2,1,0:T(8,128)(2,1)} %gather_fusion, bf16[64,128,128]{2,1,0:T(8,128)(2,1)} %gather_fusion.1, pred[64]{0:T(512)(128)(4,1)S(1)} %get-tuple-element.152, pred[64]{0:T(512)(128)(4,1)S(1)} %get-tuple-element.153), kind=kOutput, calls=%fused_computation.5.clone.1 | convolution fusion | flops 272629760 | bytes 6291584 | tf_op jit(solution)/shard_map/while/body/gxb,agb->gxa/dot_general | solution.py:46
  45.9 2.1 gather_fusion.2
  48.0 2.1 gather_fusion.3
  50.1 0.6 compare_convert_fusion.2
  50.8 5.1 %fusion.80 = f32[128,128]{1,0:T(8,128)S(1)} fusion(f32[128,128]{1,0:T(8,128)S(1)} %get-tuple-element.171, bf16[64,128,128]{2,1,0:T(8,128)(2,1)} %multiply_convert_fusion.4, bf16[64,128,128]{2,1,0:T(8,128)(2,1)} %gather_fusion.2, bf16[64,128,128]{2,1,0:T(8,128)(2,1)} %gather_fusion.3, pred[64]{0:T(512)(128)(4,1)S(1)} %get-tuple-element.156, ...), kind=kOutput, calls=%fused_computation.20.clone.1 | convolution fusion | flops 542130176 | bytes 6422784 | tf_op jit(solution)/shard_map/while/body/gxa,gay->xy/dot_general | solution.py:58
  55.9 0.8 constant_dynamic-slice_fusion.3
  56.7 2.1 gather_fusion
  58.9 2.1 gather_fusion.1
  61.0 5.2 %multiply_convert_fusion.4 = bf16[64,128,128]{2,1,0:T(8,128)(2,1)} fusion(bf16[64,128,128]{2,1,0:T(8,128)(2,1)} %gather_fusion, bf16[64,128,128]{2,1,0:T(8,128)(2,1)} %gather_fusion.1, pred[64]{0:T(512)(128)(4,1)S(1)} %get-tuple-element.152, pred[64]{0:T(512)(128)(4,1)S(1)} %get-tuple-element.153), kind=kOutput, calls=%fused_computation.5.clone.1 | convolution fusion | flops 272629760 | bytes 6291584 | tf_op jit(solution)/shard_map/while/body/gxb,agb->gxa/dot_general | solution.py:46
  66.2 2.1 gather_fusion.2
  68.3 2.1 gather_fusion.3
  70.5 0.6 compare_convert_fusion.2
  71.1 5.1 %fusion.80 = f32[128,128]{1,0:T(8,128)S(1)} fusion(f32[128,128]{1,0:T(8,128)S(1)} %get-tuple-element.171, bf16[64,128,128]{2,1,0:T(8,128)(2,1)} %multiply_convert_fusion.4, bf16[64,128,128]{2,1,0:T(8,128)(2,1)} %gather_fusion.2, bf16[64,128,128]{2,1,0:T(8,128)(2,1)} %gather_fusion.3, pred[64]{0:T(512)(128)(4,1)S(1)} %get-tuple-element.156, ...), kind=kOutput, calls=%fused_computation.20.clone.1 | convolution fusion | flops 542130176 | bytes 6422784 | tf_op jit(solution)/shard_map/while/body/gxa,gay->xy/dot_general | solution.py:58
  76.2 0.8 constant_dynamic-slice_fusion.3
  77.0 2.1 gather_fusion
  79.2 2.1 gather_fusion.1
  81.3 5.2 %multiply_convert_fusion.4 = bf16[64,128,128]{2,1,0:T(8,128)(2,1)} fusion(bf16[64,128,128]{2,1,0:T(8,128)(2,1)} %gather_fusion, bf16[64,128,128]{2,1,0:T(8,128)(2,1)} %gather_fusion.1, pred[64]{0:T(512)(128)(4,1)S(1)} %get-tuple-element.152, pred[64]{0:T(512)(128)(4,1)S(1)} %get-tuple-element.153), kind=kOutput, calls=%fused_computation.5.clone.1 | convolution fusion | flops 272629760 | bytes 6291584 | tf_op jit(solution)/shard_map/while/body/gxb,agb->gxa/dot_general | solution.py:46
  86.6 2.1 gather_fusion.2
  88.7 2.1 gather_fusion.3
  90.8 0.6 compare_convert_fusion.2
  91.5 5.1 %fusion.80 = f32[128,128]{1,0:T(8,128)S(1)} fusion(f32[128,128]{1,0:T(8,128)S(1)} %get-tuple-element.171, bf16[64,128,128]{2,1,0:T(8,128)(2,1)} %multiply_convert_fusion.4, bf16[64,128,128]{2,1,0:T(8,128)(2,1)} %gather_fusion.2, bf16[64,128,128]{2,1,0:T(8,128)(2,1)} %gather_fusion.3, pred[64]{0:T(512)(128)(4,1)S(1)} %get-tuple-element.156, ...), kind=kOutput, calls=%fused_computation.20.clone.1 | convolution fusion | flops 542130176 | bytes 6422784 | tf_op jit(solution)/shard_map/while/body/gxa,gay->xy/dot_general | solution.py:58
  96.6 0.8 constant_dynamic-slice_fusion.3
  97.4 2.1 gather_fusion
  99.6 2.1 gather_fusion.1
  101.7 5.2 %multiply_convert_fusion.4 = bf16[64,128,128]{2,1,0:T(8,128)(2,1)} fusion(bf16[64,128,128]{2,1,0:T(8,128)(2,1)} %gather_fusion, bf16[64,128,128]{2,1,0:T(8,128)(2,1)} %gather_fusion.1, pred[64]{0:T(512)(128)(4,1)S(1)} %get-tuple-element.152, pred[64]{0:T(512)(128)(4,1)S(1)} %get-tuple-element.153), kind=kOutput, calls=%fused_computation.5.clone.1 | convolution fusion | flops 272629760 | bytes 6291584 | tf_op jit(solution)/shard_map/while/body/gxb,agb->gxa/dot_general | solution.py:46
  106.9 2.1 gather_fusion.2
  109.0 2.1 gather_fusion.3
  111.2 0.6 compare_convert_fusion.2
  111.8 5.1 %fusion.80 = f32[128,128]{1,0:T(8,128)S(1)} fusion(f32[128,128]{1,0:T(8,128)S(1)} %get-tuple-element.171, bf16[64,128,128]{2,1,0:T(8,128)(2,1)} %multiply_convert_fusion.4, bf16[64,128,128]{2,1,0:T(8,128)(2,1)} %gather_fusion.2, bf16[64,128,128]{2,1,0:T(8,128)(2,1)} %gather_fusion.3, pred[64]{0:T(512)(128)(4,1)S(1)} %get-tuple-element.156, ...), kind=kOutput, calls=%fused_computation.20.clone.1 | convolution fusion | flops 542130176 | bytes 6422784 | tf_op jit(solution)/shard_map/while/body/gxa,gay->xy/dot_general | solution.py:58
  116.9 0.6 fusion.66
  117.6 100.1 %all-gather = bf16[2048,128]{1,0:T(8,128)(2,1)S(1)} all-gather(bf16[128,128]{1,0:T(8,128)(2,1)S(1)} %multiply_convert_fusion.2), channel_id=2, replica_groups=mesh['grp'=2,'had'=16] {'had'}, dimensions={0}, use_global_device_ids=true | all-gather | bytes 557056 | tf_op jit(solution)/shard_map/all_gather | solution.py:67
  217.7 0.4 fusion.35
  218.1 0.4 fusion.37
  218.5 0.9 fusion.34
  (31 shorter events, 0.2 us)
Async XLA Ops:
  0.6 1.4 copy-start
  3.3 18.6 %copy-start.2 = (s32[8,2]{0,1:T(2,128)S(1)}, s32[8,2]{0,1:T(2,128)}, u32[]{:S(2)}) copy-start(s32[8,2]{0,1:T(2,128)} %param.21) | copy-start | bytes 196
  3.3 32.2 %copy-start.1 = (bf16[16,128,128]{2,1,0:T(8,128)(2,1)S(1)}, bf16[16,128,128]{2,1,0:T(8,128)(2,1)}, u32[]{:S(2)}) copy-start(bf16[16,128,128]{2,1,0:T(8,128)(2,1)} %param.15) | copy-start | bytes 1572868
  13.8 21.7 %all-to-all-start = ((bf16[16,128,1,128]{3,1,2,0:T(8,128)(2,1)}), bf16[16,128,1,128]{3,1,2,0:T(8,128)(2,1)S(1)}, u32[]{:S(2)}, u32[]{:S(2)}) async-start(bf16[16,128,1,128]{3,1,2,0:T(8,128)(2,1)} %fusion.39), calls=%async_computation | async-start | bytes 1048576 | tf_op jit(solution)/shard_map/all_to_all | solution.py:34
